TPU v7x, 512 devices: a whole 4x4x16 slice. The times are simulated.
512 devices in a mesh: rep: 128 (over x, y_lo, z), dp: 4 (over y_hi, core).
Axes of the slice: x: 4, y: 4 (y_hi: 2, y_lo: 2; y = y_hi * 2 + y_lo), z: 16, core: 2. Of those that a mesh axis runs over, the one named last changes fastest.
Arguments:
- residual_flow: bfloat16 [1536, 1024], P('dp'), may hold values from -6 to 6
- rooted_input_matrix: bfloat16 [128, 1024, 2048], P('rep', None, 'dp'), may hold values from -6 to 6
- chain_normal_draws: bfloat16 [128, 1024, 2048], P('rep', None, 'dp'), may hold values from -6 to 6
- output_matrix: bfloat16 [2048, 1024], P('dp'), may hold values from -0.125 to 0.125
- chain_heat: float32 [128], P('rep'), may hold values from 0.05 to 1
- matched_chain: int32 [128], P('rep'), may hold values from 0 to 127, as said below
- swap_mask: int32 [128], P('rep'), may hold values from 0 to 1, as said below
Outputs:
- swapped: bfloat16 [128, 1024, 2048], P('rep', None, 'dp')
- chain_gaps: float32 [128, 2, 2048], P('rep', None, 'dp')
Inputs may be any that keep to these rules, and one draw needn't show every extreme that they name: Replicas form aligned blocks of four; in each block one of these holds: 4b with 4b + 1 and 4b + 2 with 4b + 3 are mates; only 4b + 1 with 4b + 2; only 4b with 4b + 1; only 4b + 2 with 4b + 3. matched_chain[r] is r's mate, or r where r has none. `swap_mask`: mates carry the same flag; a replica without a mate carries 0; every matched pair of the first block carries 1.
All inputs are finite; a program needn't handle non-finite values.
Results may differ from a plain program's by a relative error of at most 0.014.
Values may be sent and summed in bfloat16 or wider, within the bound.
A program may use at most 64 MiB of HBM per device.

v0:
```python
import math

import jax
import jax.numpy as jnp
from jax import lax
from jax.sharding import PartitionSpec as P

drift_stride = 0.5


def shifted(value, axis, steps):
    count = lax.axis_size(axis)
    pairs = [(source, (source + steps) % count) for source in range(count)]
    return lax.ppermute(value, axis, pairs)


def normalize(residual_flow):
    values = residual_flow.astype(jnp.float32)
    center = values - jnp.mean(values, axis=1, keepdims=True)
    spread = jnp.mean(center * center, axis=1, keepdims=True)
    return (center * lax.rsqrt(spread + 1e-05)).astype(jnp.bfloat16)


def gelu_value(values):
    inner = math.sqrt(2.0 / math.pi) * (values + 0.044715 * values * values * values)
    return 0.5 * values * (1.0 + jnp.tanh(inner))


def gelu_slope(values):
    coeff = math.sqrt(2.0 / math.pi)
    inner = coeff * (values + 0.044715 * values * values * values)
    tangent = jnp.tanh(inner)
    return 0.5 * (1.0 + tangent) + 0.5 * values * (1.0 - tangent * tangent) * coeff * (
        1.0 + 3.0 * 0.044715 * values * values
    )


def next_errors(output, residual_flow):
    width = residual_flow.shape[1]
    ahead = output[:-1] - residual_flow[1:].astype(jnp.float32)
    return jnp.concatenate([ahead, jnp.zeros((1, width), jnp.float32)], axis=0).astype(jnp.bfloat16)


def against_rows(errors, weight):
    return lax.dot_general(
        errors, weight, (((1,), (1,)), ((), ())), preferred_element_type=jnp.float32
    )


def body(
    residual_flow,
    rooted_input_matrix,
    chain_normal_draws,
    output_matrix,
    chain_heat,
    matched_chain,
    swap_mask,
):
    width = rooted_input_matrix.shape[1]
    factor = width ** (-0.5)
    normed = normalize(residual_flow)
    params = rooted_input_matrix[0]
    preact = (
        jnp.dot(
            normed,
            lax.all_gather(params, "dp", axis=1, tiled=True),
            preferred_element_type=jnp.float32,
        )
        * factor
    )
    down_full = lax.all_gather(output_matrix, "dp", axis=0, tiled=True)
    hidden = gelu_value(preact).astype(jnp.bfloat16)
    output = residual_flow.astype(jnp.float32) + jnp.dot(
        hidden, down_full, preferred_element_type=jnp.float32
    )
    errors = next_errors(output, residual_flow)
    hidden_grad = against_rows(errors, down_full)
    preact_grad = (hidden_grad * gelu_slope(preact)).astype(jnp.bfloat16)
    partial_value = (
        lax.dot_general(
            normed, preact_grad, (((0,), (0,)), ((), ())), preferred_element_type=jnp.float32
        )
        * factor
    )
    gradient = lax.psum_scatter(
        partial_value.astype(jnp.bfloat16), "dp", scatter_dimension=1, tiled=True
    ).astype(jnp.float32)
    current = params.astype(jnp.float32)
    moved = (
        current
        - drift_stride * (gradient + current)
        + jnp.sqrt(2.0 * drift_stride * chain_heat[0]) * chain_normal_draws[0].astype(jnp.float32)
    )
    refreshed_input_matrix = moved.astype(jnp.bfloat16)
    own_rank = lax.axis_index("rep")
    mate = matched_chain[0]
    taken = swap_mask[0] == 1
    below = shifted(refreshed_input_matrix, "rep", 1)
    above = shifted(refreshed_input_matrix, "rep", -1)
    result = jnp.where(
        taken & (mate == own_rank - 1),
        below,
        jnp.where(taken & (mate == own_rank + 1), above, refreshed_input_matrix),
    )
    own_values = refreshed_input_matrix.astype(jnp.float32)
    lower_diff = own_values - below.astype(jnp.float32)
    upper_diff = own_values - above.astype(jnp.float32)
    chain_gaps = jnp.stack(
        [jnp.mean(lower_diff * lower_diff, axis=0), jnp.mean(upper_diff * upper_diff, axis=0)],
        axis=0,
    )
    return (result[None], chain_gaps[None])


def solution(mesh):
    placed = (
        P("dp", None),
        P("rep", None, "dp"),
        P("rep", None, "dp"),
        P("dp", None),
        P("rep"),
        P("rep"),
        P("rep"),
    )
    return jax.shard_map(
        body,
        mesh=mesh,
        in_specs=placed,
        out_specs=(P("rep", None, "dp"), P("rep", None, "dp")),
        check_vma=False,
    )
```

profile of v0, /device:TPU:1, one launch (start us, length us, event | category | flops | bytes accessed | tf_op | source)
XLA Modules:
  0.0 233.2 jit_solution(10997246936140800611)
XLA Ops:
  7.2 0.0 all-gather.6.cloned.1.call-start
  7.2 0.7 all-gather.6.cloned.1.call-update
  7.9 0.0 all-gather.4.cloned.1.call-start
  8.0 0.7 all-gather.4.cloned.1.call-update
  8.7 0.0 reduce-scatter.2.cloned.1.call-start
  8.7 1.3 convert_element_type.43
  10.0 0.2 convert_reduce_fusion
  10.2 0.3 multiply_reduce_fusion
  10.6 51.5 %all-gather.6.cloned.1.call-done = bf16[1,1024,2048]{2,1,0:T(8,128)(2,1)} async-done(((bf16[1,1024,512]{2,1,0:T(8,128)(2,1)}), bf16[1,1024,2048]{2,1,0:T(8,128)(2,1)}) %all-gather.6.cloned.1.call-update) | async-done | bytes 4194320 | tf_op jit(solution)/shard_map/all_gather | solution.py:66
  62.1 5.8 %fusion = f32[384,2048]{1,0:T(8,128)} fusion(bf16[1,1024,2048]{2,1,0:T(8,128)(2,1)} %all-gather.6.cloned.1.call-done, bf16[384,1024]{1,0:T(8,128)(2,1)S(1)} %copy-done, f32[384]{0:T(512)S(1)} %add_rsqrt_fusion, f32[384]{0:T(512)S(1)} %broadcast_multiply_fusion.2), kind=kOutput, calls=%fused_computation.2 | convolution fusion | flops 1612185600 | bytes 8129536 | tf_op jit(solution)/shard_map/dot_general | solution.py:64
  67.9 42.0 %all-gather.4.cloned.1.call-done = bf16[2048,1024]{1,0:T(8,128)(2,1)} async-done(((bf16[512,1024]{1,0:T(8,128)(2,1)}), bf16[2048,1024]{1,0:T(8,128)(2,1)}) %all-gather.4.cloned.1.call-update) | async-done | bytes 4194320 | tf_op jit(solution)/shard_map/all_gather | solution.py:71
  109.9 5.3 %fusion.12 = f32[384,1024]{1,0:T(8,128)S(1)} fusion(bf16[2048,1024]{1,0:T(8,128)(2,1)} %all-gather.4.cloned.1.call-done, f32[384,2048]{1,0:T(8,128)} %fusion), kind=kOutput, calls=%fused_computation.20 | convolution fusion | flops 1618477056 | bytes 8912896 | tf_op jit(solution)/shard_map/dot_general | solution.py:73
  115.2 0.5 fusion.14
  115.6 9.2 %multiply_convert_fusion = bf16[1024,2048]{1,0:T(8,128)(2,1)} fusion(f32[384,2048]{1,0:T(8,128)} %fusion, bf16[2048,1024]{1,0:T(8,128)(2,1)} %all-gather.4.cloned.1.call-done, bf16[383,1024]{1,0:T(8,128)(2,1)S(1)} %fusion.14, bf16[384,1024]{1,0:T(8,128)(2,1)S(1)} %copy-done, f32[384]{0:T(512)S(1)} %add_rsqrt_fusion, f32[384]{0:T(512)S(1)} %broadcast_multiply_fusion.2), kind=kOutput, calls=%fused_computation | convolution fusion | flops 3242721280 | bytes 13108224 | tf_op jit(solution)/shard_map/dot_general | solution.py:80
  124.9 0.0 reduce-scatter.2.cloned.1.call-update
  125.7 65.3 %reduce-scatter.2.cloned.1.call-done = bf16[1024,512]{1,0:T(8,128)(2,1)} async-done(((bf16[1024,2048]{1,0:T(8,128)(2,1)}), bf16[1024,512]{1,0:T(8,128)(2,1)}) %reduce-scatter.2.cloned.1.call-update) | async-done | bytes 1048592 | tf_op jit(solution)/shard_map/reduce_scatter | solution.py:85
  191.0 1.8 fusion.11
  192.8 3.2 %collective-permute-start = (bf16[1024,512]{1,0:T(8,128)(2,1)S(1)}, bf16[1024,512]{1,0:T(8,128)(2,1)S(1)}, u32[]{:S(2)}, u32[]{:S(2)}) collective-permute-start(bf16[1024,512]{1,0:T(8,128)(2,1)S(1)} %fusion.11), channel_id=1, source_target_pairs={{0,4},{4,8},{8,12},{12,16},{16,20},{20,24},{24,28},{28,32},{32,36}... | collective-permute-start | bytes 3145736 | tf_op jit(solution)/shard_map/ppermute | solution.py:14
  196.0 6.6 %collective-permute-start.1 = (bf16[1024,512]{1,0:T(8,128)(2,1)S(1)}, bf16[1024,512]{1,0:T(8,128)(2,1)S(1)}, u32[]{:S(2)}, u32[]{:S(2)}) collective-permute-start(bf16[1024,512]{1,0:T(8,128)(2,1)S(1)} %fusion.11), channel_id=1, source_target_pairs={{0,508},{4,0},{8,4},{12,8},{16,12},{20,16},{24,20},{28,24},{32,28}... | collective-permute-start | bytes 3145736 | tf_op jit(solution)/shard_map/ppermute | solution.py:14
  203.9 19.6 %collective-permute-done = bf16[1024,512]{1,0:T(8,128)(2,1)S(1)} collective-permute-done((bf16[1024,512]{1,0:T(8,128)(2,1)S(1)}, bf16[1024,512]{1,0:T(8,128)(2,1)S(1)}, u32[]{:S(2)}, u32[]{:S(2)}) %collective-permute-start) | collective-permute-done | bytes 1048608 | tf_op jit(solution)/shard_map/ppermute | solution.py:14
  223.5 0.9 collective-permute-done.1
  224.3 0.6 fusion.6
  225.0 0.6 maximum_bitcast_fusion
  225.6 1.1 select_bitcast_fusion
  (9 shorter events, 0.0 us)
Async XLA Ops:
  7.2 2.8 %copy-start = (bf16[384,1024]{1,0:T(8,128)(2,1)S(1)}, bf16[384,1024]{1,0:T(8,128)(2,1)}, u32[]{:S(2)}) copy-start(bf16[384,1024]{1,0:T(8,128)(2,1)} %param.7) | copy-start | bytes 2359300
  7.2 54.9 %all-gather.6.cloned.1.call-start = ((), (), s32[]{:S(2)}) async-start(), calls=%async_computation.3 | async-start | bytes 5242880 | tf_op jit(solution)/shard_map/all_gather | solution.py:66
  7.9 102.0 %all-gather.4.cloned.1.call-start = ((), (), s32[]{:S(2)}) async-start(), calls=%async_computation.1 | async-start | bytes 5242880 | tf_op jit(solution)/shard_map/all_gather | solution.py:71
  8.7 182.4 %reduce-scatter.2.cloned.1.call-start = ((), (), s32[]{:S(2)}) async-start(), calls=%async_computation.2 | async-start | bytes 5242880 | tf_op jit(solution)/shard_map/reduce_scatter | solution.py:85
  124.9 66.1 %copy-start.1 = (bf16[1,1024,512]{2,1,0:T(8,128)(2,1)S(1)}, bf16[1,1024,512]{2,1,0:T(8,128)(2,1)}, u32[]{:S(2)}) copy-start(bf16[1,1024,512]{2,1,0:T(8,128)(2,1)} %param.8) | copy-start | bytes 3145732
  124.9 66.1 %copy-start.2 = (bf16[1,1024,512]{2,1,0:T(8,128)(2,1)S(1)}, bf16[1,1024,512]{2,1,0:T(8,128)(2,1)}, u32[]{:S(2)}) copy-start(bf16[1,1024,512]{2,1,0:T(8,128)(2,1)} %param.9) | copy-start | bytes 3145732
  192.8 30.6 %collective-permute-start = (bf16[1024,512]{1,0:T(8,128)(2,1)S(1)}, bf16[1024,512]{1,0:T(8,128)(2,1)S(1)}, u32[]{:S(2)}, u32[]{:S(2)}) collective-permute-start(bf16[1024,512]{1,0:T(8,128)(2,1)S(1)} %fusion.11), channel_id=1, source_target_pairs={{0,4},{4,8},{8,12},{12,16},{16,20},{20,24},{24,28},{28,32},{32,36}... | collective-permute-start | bytes 3145736 | tf_op jit(solution)/shard_map/ppermute | solution.py:14
  196.0 28.3 %collective-permute-start.1 = (bf16[1024,512]{1,0:T(8,128)(2,1)S(1)}, bf16[1024,512]{1,0:T(8,128)(2,1)S(1)}, u32[]{:S(2)}, u32[]{:S(2)}) collective-permute-start(bf16[1024,512]{1,0:T(8,128)(2,1)S(1)} %fusion.11), channel_id=1, source_target_pairs={{0,508},{4,0},{8,4},{12,8},{16,12},{20,16},{24,20},{28,24},{32,28}... | collective-permute-start | bytes 3145736 | tf_op jit(solution)/shard_map/ppermute | solution.py:14
Sparse Core Ops, SparseCore 0:
  10.1 51.9 all-gather.5
  64.2 45.6 all-gather.3
  125.0 65.9 reduce-scatter.1
where the time goes:
time: 233 us
  waiting for transfers between devices  181 us (78%)
  matrix products  20.3 us (9%)
  between operations  15.9 us (7%)
  starting transfers between devices  9.84 us (4%)
  other arithmetic  6.44 us (3%)
    reduce_scatter x1, waiting for transfers between devices, body(): lax.psum_scatter(partial_value.astype(jnp.bfloat16), 'dp', scatter_dimens...  65.3 us
    all_gather x1, waiting for transfers between devices, body(): lax.all_gather(params, 'dp', axis=1, tiled=True)  51.5 us
    all_gather x1, waiting for transfers between devices, body(): down_full = lax.all_gather(output_matrix, 'dp', axis=0, tiled=True)  42 us
    ppermute x2, waiting for transfers between devices, shifted(): return lax.ppermute(value, axis, pairs)  20.4 us
    ppermute x2, starting transfers between devices, shifted(): return lax.ppermute(value, axis, pairs)  9.72 us
    dot_general x1, matrix products, body(): lax.dot_general(normed, preact_grad, (((0,), (0,)), ((), ())), preferred_...  9.25 us
    dot_general x1, matrix products, body(): jnp.dot(normed, lax.all_gather(params, 'dp', axis=1, tiled=True), preferr...  5.84 us
    dot_general x1, matrix products, body(): jnp.dot(hidden, down_full, preferred_element_type=jnp.float32)  5.26 us
  transfers between devices with their start and end apart: 5, of which 5 were waited for; matrix products, arithmetic and copies ran while one was open for 3% of the time, Pallas kernels for 0%

commit v1 on v0

--- a/solution.py
+++ b/solution.py
@@ -58,33 +58,23 @@
 ):
     width = rooted_input_matrix.shape[1]
     factor = width ** (-0.5)
-    normed = normalize(residual_flow)
     params = rooted_input_matrix[0]
-    preact = (
-        jnp.dot(
-            normed,
-            lax.all_gather(params, "dp", axis=1, tiled=True),
-            preferred_element_type=jnp.float32,
-        )
-        * factor
-    )
-    down_full = lax.all_gather(output_matrix, "dp", axis=0, tiled=True)
+    normed = lax.all_gather(normalize(residual_flow), "dp", axis=0, tiled=True)
+    preact = jnp.dot(normed, params, preferred_element_type=jnp.float32) * factor
     hidden = gelu_value(preact).astype(jnp.bfloat16)
-    output = residual_flow.astype(jnp.float32) + jnp.dot(
-        hidden, down_full, preferred_element_type=jnp.float32
-    )
-    errors = next_errors(output, residual_flow)
-    hidden_grad = against_rows(errors, down_full)
+    part = jnp.dot(hidden, output_matrix, preferred_element_type=jnp.float32)
+    own = residual_flow.astype(jnp.float32) + lax.psum_scatter(
+        part.astype(jnp.bfloat16), "dp", scatter_dimension=0, tiled=True
+    ).astype(jnp.float32)
+    errors = lax.all_gather(next_errors(own, residual_flow), "dp", axis=0, tiled=True)
+    hidden_grad = against_rows(errors, output_matrix)
     preact_grad = (hidden_grad * gelu_slope(preact)).astype(jnp.bfloat16)
-    partial_value = (
+    gradient = (
         lax.dot_general(
             normed, preact_grad, (((0,), (0,)), ((), ())), preferred_element_type=jnp.float32
         )
         * factor
     )
-    gradient = lax.psum_scatter(
-        partial_value.astype(jnp.bfloat16), "dp", scatter_dimension=1, tiled=True
-    ).astype(jnp.float32)
     current = params.astype(jnp.float32)
     moved = (
         current

time: 233 us -> 222 us (0.953)
  waiting for transfers between devices: 181 us -> 165 us
  other arithmetic: 6.44 us -> 10.5 us
  local copies, waits for them, and re-layouts: 0.01 us -> 3.69 us
  matrix products: 20.3 us -> 16.8 us
    all_gather x2, waiting for transfers between devices: 93.5 us -> 86 us  [the longest x1 46.1 us: body(): normed = lax.all_gather(normalize(residual_flow), 'dp', axis=0, tiled=True)]
    reduce_scatter x1, waiting for transfers between devices: 65.3 us -> 58.3 us  [body(): lax.psum_scatter(part.astype(jnp.bfloat16), 'dp', scatter_dimension=0, ti...]
    dot_general x2, matrix products: 11.1 us -> 7.63 us  [the longest x1 3.91 us: body(): part = jnp.dot(hidden, output_matrix, preferred_element_type=jnp.float32)]
    unnamed x6 -> x8, local copies, waits for them, and re-layouts: 0.01 us -> 2.75 us
  transfers between devices with their start and end apart: 5 -> 5, of which waited for: 5 -> 5; matrix products, arithmetic and copies ran while one was open for 3% -> 0% of each run, Pallas kernels for 0% -> 0%
where the time goes in v1:
time: 222 us
  waiting for transfers between devices  165 us (74%)
  matrix products  16.8 us (8%)
  between operations  15.8 us (7%)
  other arithmetic  10.5 us (5%)
  starting transfers between devices  9.85 us (4%)
  local copies, waits for them, and re-layouts  3.69 us (2%)
    reduce_scatter x1, waiting for transfers between devices, body(): lax.psum_scatter(part.astype(jnp.bfloat16), 'dp', scatter_dimension=0, ti...  58.3 us
    all_gather x1, waiting for transfers between devices, body(): normed = lax.all_gather(normalize(residual_flow), 'dp', axis=0, tiled=True)  46.1 us
    all_gather x1, waiting for transfers between devices, body(): lax.all_gather(next_errors(own, residual_flow), 'dp', axis=0, tiled=True)  39.9 us
    ppermute x2, waiting for transfers between devices, shifted(): return lax.ppermute(value, axis, pairs)  20.9 us
    ppermute x2, starting transfers between devices, shifted(): return lax.ppermute(value, axis, pairs)  9.73 us
    dot_general x1, matrix products, body(): lax.dot_general(normed, preact_grad, (((0,), (0,)), ((), ())), preferred_...  9.2 us
  transfers between devices with their start and end apart: 5, of which 5 were waited for; matrix products, arithmetic and copies ran while one was open for 0% of the time, Pallas kernels for 0%

profile of v1, /device:TPU:1, one launch (start us, length us, event | category | flops | bytes accessed | tf_op | source)
XLA Modules:
  0.0 221.9 jit_solution(18027995805339141520)
XLA Ops:
  7.2 0.0 all-gather.3.cloned.1.call-start
  7.2 1.5 convert_reduce_fusion
  8.7 1.5 multiply_reduce_fusion
  10.2 2.3 %multiply_convert_fusion.2 = bf16[384,1024]{1,0:T(8,128)(2,1)} fusion(bf16[384,1024]{1,0:T(8,128)(2,1)} %param.7, f32[384]{0:T(512)S(1)} %add_rsqrt_fusion, f32[384]{0:T(512)S(1)} %broadcast_multiply_fusion.2), kind=kLoop, calls=%fused_computation.35 | loop fusion | flops 1572864 | bytes 1575936 | tf_op jit(solution)/shard_map/convert_element_type | solution.py:21
  12.5 0.0 reduce-scatter.2.cloned.1.call-start
  12.5 46.1 %all-gather.3.cloned.1.call-done = bf16[1536,1024]{1,0:T(8,128)(2,1)} async-done(((bf16[384,1024]{1,0:T(8,128)(2,1)}), bf16[1536,1024]{1,0:T(8,128)(2,1)}) %all-gather.3.cloned.1.call-update) | async-done | bytes 3145744 | tf_op jit(solution)/shard_map/all_gather | solution.py:62
  58.6 3.7 %fusion.26 = f32[1536,512]{1,0:T(8,128)S(1)} fusion(bf16[1536,1024]{1,0:T(8,128)(2,1)} %all-gather.3.cloned.1.call-done, bf16[1,1024,512]{2,1,0:T(8,128)(2,1)S(1)} %copy-done.2), kind=kOutput, calls=%fused_computation.38 | convolution fusion | flops 1610612736 | bytes 7340032 | tf_op jit(solution)/shard_map/dot_general | solution.py:63
  62.4 1.7 copy-done.3
  64.0 3.9 %convolution_convert_fusion = bf16[1536,1024]{1,0:T(8,128)(2,1)} fusion(bf16[512,1024]{1,0:T(8,128)(2,1)S(1)} %copy-done, f32[1536,512]{1,0:T(8,128)S(1)} %fusion.26), kind=kOutput, calls=%fused_computation.1 | convolution fusion | flops 1620049920 | bytes 7340032 | tf_op jit(solution)/shard_map/dot_general | solution.py:65
  68.0 0.0 all-gather.5.cloned.1.call-start
  68.0 1.1 copy-done.1
  69.1 0.2 convert_element_type.43
  69.2 58.3 %reduce-scatter.2.cloned.1.call-done = bf16[384,1024]{1,0:T(8,128)(2,1)} async-done(((bf16[1536,1024]{1,0:T(8,128)(2,1)}), bf16[384,1024]{1,0:T(8,128)(2,1)}) %reduce-scatter.2.cloned.1.call-update) | async-done | bytes 786448 | tf_op jit(solution)/shard_map/reduce_scatter | solution.py:66
  127.5 1.5 fusion.13
  129.0 0.9 concatenate.3
  130.7 39.9 %all-gather.5.cloned.1.call-done = bf16[1536,1024]{1,0:T(8,128)(2,1)} async-done(((bf16[384,1024]{1,0:T(8,128)(2,1)}), bf16[1536,1024]{1,0:T(8,128)(2,1)}) %all-gather.5.cloned.1.call-update) | async-done | bytes 3145744 | tf_op jit(solution)/shard_map/all_gather | solution.py:69
  170.6 9.2 %fusion.6 = bf16[1024,512]{1,0:T(8,128)(2,1)S(1)} fusion(bf16[1,1024,512]{2,1,0:T(8,128)(2,1)} %param.9, bf16[1536,1024]{1,0:T(8,128)(2,1)} %all-gather.3.cloned.1.call-done, f32[1536,512]{1,0:T(8,128)} %copy-done.3, bf16[1536,1024]{1,0:T(8,128)(2,1)} %all-gather.5.cloned.1.call-done, bf16[512,1024]{1,0:T(8,128)(2,1)S(1)} %copy-done, ...), kind=kOutput, calls=%fused_computation.14 | convolution fusion | flops 3241672704 | bytes 13631492 | tf_op jit(solution)/shard_map/dot_general | solution.py:73
  179.8 3.2 %collective-permute-start = (bf16[1024,512]{1,0:T(8,128)(2,1)S(1)}, bf16[1024,512]{1,0:T(8,128)(2,1)S(1)}, u32[]{:S(2)}, u32[]{:S(2)}) collective-permute-start(bf16[1024,512]{1,0:T(8,128)(2,1)S(1)} %fusion.6), channel_id=1, source_target_pairs={{0,4},{4,8},{8,12},{12,16},{16,20},{20,24},{24,28},{28,32},{32,36}... | collective-permute-start | bytes 3145736 | tf_op jit(solution)/shard_map/ppermute | solution.py:14
  182.9 6.6 %collective-permute-start.1 = (bf16[1024,512]{1,0:T(8,128)(2,1)S(1)}, bf16[1024,512]{1,0:T(8,128)(2,1)}, u32[]{:S(2)}, u32[]{:S(2)}) collective-permute-start(bf16[1024,512]{1,0:T(8,128)(2,1)S(1)} %fusion.6), channel_id=1, source_target_pairs={{0,508},{4,0},{8,4},{12,8},{16,12},{20,16},{24,20},{28,24},{32,28}... | collective-permute-start | bytes 3145736 | tf_op jit(solution)/shard_map/ppermute | solution.py:14
  190.8 20.1 %collective-permute-done = bf16[1024,512]{1,0:T(8,128)(2,1)S(1)} collective-permute-done((bf16[1024,512]{1,0:T(8,128)(2,1)S(1)}, bf16[1024,512]{1,0:T(8,128)(2,1)S(1)}, u32[]{:S(2)}, u32[]{:S(2)}) %collective-permute-start) | collective-permute-done | bytes 1048608 | tf_op jit(solution)/shard_map/ppermute | solution.py:14
  210.9 0.9 collective-permute-done.1
  211.8 1.8 fusion.8
  213.6 0.6 maximum_bitcast_fusion
  214.2 1.1 select_bitcast_fusion
  (12 shorter events, 0.1 us)
Async XLA Ops:
  7.2 56.9 %copy-start = (bf16[512,1024]{1,0:T(8,128)(2,1)S(1)}, bf16[512,1024]{1,0:T(8,128)(2,1)}, u32[]{:S(2)}) copy-start(bf16[512,1024]{1,0:T(8,128)(2,1)} %param.10) | copy-start | bytes 3145732
  7.2 51.4 %copy-start.2 = (bf16[1,1024,512]{2,1,0:T(8,128)(2,1)S(1)}, bf16[1,1024,512]{2,1,0:T(8,128)(2,1)}, u32[]{:S(2)}) copy-start(bf16[1,1024,512]{2,1,0:T(8,128)(2,1)} %param.8) | copy-start | bytes 3145732
  7.2 51.4 %all-gather.3.cloned.1.call-start = ((), (), s32[]{:S(2)}) async-start(), calls=%async_computation.1 | async-start | bytes 3932160 | tf_op jit(solution)/shard_map/all_gather | solution.py:62
  12.5 115.0 %reduce-scatter.2.cloned.1.call-start = ((), (), s32[]{:S(2)}) async-start(), calls=%async_computation.2 | async-start | bytes 3932160 | tf_op jit(solution)/shard_map/reduce_scatter | solution.py:66
  62.3 1.7 copy-start.3
  67.9 1.1 copy-start.1
  68.0 102.6 %all-gather.5.cloned.1.call-start = ((), (), s32[]{:S(2)}) async-start(), calls=%async_computation.3 | async-start | bytes 3932160 | tf_op jit(solution)/shard_map/all_gather | solution.py:69
  179.8 31.1 %collective-permute-start = (bf16[1024,512]{1,0:T(8,128)(2,1)S(1)}, bf16[1024,512]{1,0:T(8,128)(2,1)S(1)}, u32[]{:S(2)}, u32[]{:S(2)}) collective-permute-start(bf16[1024,512]{1,0:T(8,128)(2,1)S(1)} %fusion.6), channel_id=1, source_target_pairs={{0,4},{4,8},{8,12},{12,16},{16,20},{20,24},{24,28},{28,32},{32,36}... | collective-permute-start | bytes 3145736 | tf_op jit(solution)/shard_map/ppermute | solution.py:14
  182.9 28.8 %collective-permute-start.1 = (bf16[1024,512]{1,0:T(8,128)(2,1)S(1)}, bf16[1024,512]{1,0:T(8,128)(2,1)}, u32[]{:S(2)}, u32[]{:S(2)}) collective-permute-start(bf16[1024,512]{1,0:T(8,128)(2,1)S(1)} %fusion.6), channel_id=1, source_target_pairs={{0,508},{4,0},{8,4},{12,8},{16,12},{20,16},{24,20},{28,24},{32,28}... | collective-permute-start | bytes 3145736 | tf_op jit(solution)/shard_map/ppermute | solution.py:14
Sparse Core Ops, SparseCore 0:
  12.6 45.9 all-gather.2
  68.1 59.3 reduce-scatter.1
  130.4 40.1 all-gather.4

commit v2 on v1

v2 whole, which is shorter than its diff:
```python
import functools
import math

import jax
import jax.numpy as jnp
from jax import lax
from jax.experimental import pallas as pl
from jax.experimental.pallas import tpu as pltpu
from jax.sharding import PartitionSpec as P

MESH = pl.DeviceIdType.MESH
drift_stride = 0.5
TILE = 128
CHUNK = 256


def place():
    rep = lax.axis_index("rep")
    dp = lax.axis_index("dp")
    return rep, rep // 32, (rep // 16) % 2, rep % 16, dp // 2, dp % 2


def peers():
    rep, x, y_lo, z, y_hi, core = place()
    dp = y_hi * 2 + core

    def at(x, y_lo, y_hi, core):
        return ((x * 2 + y_lo) * 16 + z, y_hi * 2 + core)

    return {
        "sibling": at(x, y_lo, y_hi, 1 - core),
        "partner": at(x, y_lo, 1 - y_hi, core),
        "across": at(x, 1 - y_lo, 1 - y_hi, core),
        "x1": at((x + 1) % 4, y_lo, y_hi, core),
        "x2": at((x + 2) % 4, y_lo, y_hi, core),
        "x3": at((x + 3) % 4, y_lo, y_hi, core),
        "up": ((rep + 1) % 128, dp),
        "down": ((rep + 127) % 128, dp),
    }


def kernel(
    res_hbm,
    par_hbm,
    noise_hbm,
    down_hbm,
    heat,
    mate,
    mask,
    out_ref,
    gap_ref,
    res,
    par,
    noise,
    down,
    nrm,
    flip,
    flip_sib,
    slope,
    base,
    op_send,
    op_recv,
    hid,
    pg_send,
    pg_own,
    pg_sib,
    acc,
    rest,
    fresh,
    near,
    load_sem,
    swap_s,
    swap_r,
    quart_s,
    quart_r,
    spread_s,
    spread_r,
    flip_s,
    flip_r,
    op_s,
    op_r,
    pg_s,
    pg_r,
    z_s,
    z_r,
):
    factor = 1024 ** (-0.5)
    coeff = math.sqrt(2.0 / math.pi)
    rank, x = place()[:2]
    peer = peers()

    def remote(src, dst, send, recv, who):
        return pltpu.make_async_remote_copy(
            src_ref=src,
            dst_ref=dst,
            send_sem=send,
            recv_sem=recv,
            device_id=peer[who],
            device_id_type=MESH,
        )

    loads = [
        pltpu.make_async_copy(res_hbm, res.at[0], load_sem.at[0]),
        pltpu.make_async_copy(par_hbm.at[0], par.at[0], load_sem.at[1]),
        pltpu.make_async_copy(down_hbm, down.at[0], load_sem.at[2]),
        pltpu.make_async_copy(noise_hbm.at[0], noise, load_sem.at[3]),
    ]
    for copy in loads:
        copy.start()

    barrier = pltpu.get_barrier_semaphore()
    for who in peer:
        pl.semaphore_signal(barrier, inc=1, device_id=peer[who], device_id_type=MESH)
    pl.semaphore_wait(barrier, len(peer))

    quarter = pl.ds(pl.multiple_of(x * 96, 96), 96)
    loads[0].wait()
    quart = remote(res.at[0, quarter], res.at[1, quarter], quart_s, quart_r, "across")
    quart.start()
    loads[1].wait()
    swap_par = remote(par.at[0], par.at[1], swap_s.at[0], swap_r.at[0], "sibling")
    swap_par.start()
    loads[2].wait()
    swap_down = remote(down.at[0], down.at[1], swap_s.at[1], swap_r.at[1], "sibling")
    swap_down.start()

    def flip_copy(j):
        return remote(flip.at[j], flip_sib.at[j], flip_s.at[j], flip_r.at[j], "sibling")

    def op_copy(j):
        return remote(
            op_send.at[j], op_recv.at[(j + 3) % 6], op_s.at[j], op_r.at[(j + 3) % 6], "partner"
        )

    def pg_copy(j):
        return remote(pg_send.at[j], pg_sib.at[j], pg_s.at[j], pg_r.at[j], "sibling")

    def prepare(seq):
        def one(k, _):
            rows = pl.ds(pl.multiple_of(k * TILE, TILE), TILE)
            values = res[seq, rows, :].astype(jnp.float32)
            center = values - jnp.mean(values, axis=1, keepdims=True)
            spread = jnp.mean(center * center, axis=1, keepdims=True)
            nrm[seq * 3 + k] = (center * lax.rsqrt(spread + 1e-05)).astype(jnp.bfloat16)
            return 0

        lax.fori_loop(0, 3, one, 0)

    def step_ahead(seq):
        for c in range(4):
            cols = slice(c * CHUNK, (c + 1) * CHUNK)
            values = res[seq, :, cols].astype(jnp.float32)
            ahead = values - pltpu.roll(values, 383, 0)
            for k in range(3):
                base[seq * 3 + k, :, cols] = ahead[k * TILE : (k + 1) * TILE]

    def forward(j, _):
        rows = nrm[j]
        for c in range(4):
            cols = slice((c % 2) * CHUNK, (c % 2 + 1) * CHUNK)
            wide = slice(c * CHUNK, (c + 1) * CHUNK)
            v = jnp.dot(rows, par[c // 2, :, cols], preferred_element_type=jnp.float32) * factor
            square = v * v
            tangent = jnp.tanh(coeff * v * (1.0 + 0.044715 * square))
            half = 0.5 * (1.0 + tangent)
            hid[:, wide] = (v * half).astype(jnp.bfloat16)
            slope[j, :, wide] = half + 0.5 * coeff * v * (1.0 - tangent * tangent) * (
                1.0 + 3.0 * 0.044715 * square
            )
        for c in range(4):
            wide = slice(c * CHUNK, (c + 1) * CHUNK)
            part = jnp.dot(
                hid[:, :512], down[0, :, wide], preferred_element_type=jnp.float32
            ) + jnp.dot(hid[:, 512:], down[1, :, wide], preferred_element_type=jnp.float32)
            base[j, :, wide] += part
            op_send[j, :, wide] = part.astype(jnp.bfloat16)
        op_copy(j).start()
        return 0

    def turn(j, _):
        flip[j] = nrm[j].T
        flip_copy(j).start()
        return 0

    prepare(0)
    step_ahead(0)
    swap_par.wait_recv()
    swap_down.wait_recv()
    quart.wait_recv()
    spreads = [
        remote(
            res.at[1, quarter], res.at[1, quarter], spread_s.at[k - 1], spread_r.at[k - 1], f"x{k}"
        )
        for k in (1, 2, 3)
    ]
    for copy in spreads:
        copy.start()
    lax.fori_loop(0, 3, forward, 0)
    lax.fori_loop(0, 3, turn, 0)

    loads[3].wait()
    heat_root = jnp.sqrt(jnp.full((1, 512), 2.0 * drift_stride * heat[0], jnp.float32))

    def keep(k, _):
        rows = pl.ds(pl.multiple_of(k * TILE, TILE), TILE)
        current = par[0, rows, :].astype(jnp.float32)
        rest[rows, :] = (
            current - drift_stride * current + heat_root * noise[rows, :].astype(jnp.float32)
        )
        acc[rows, :] = jnp.zeros((TILE, 512), jnp.float32)
        return 0

    lax.fori_loop(0, 8, keep, 0)

    for copy in spreads:
        copy.wait_recv()
    prepare(1)
    step_ahead(1)
    lax.fori_loop(3, 6, forward, 0)
    lax.fori_loop(3, 6, turn, 0)

    def backward(j):
        op_copy((j + 3) % 6).wait_recv()
        keepers = lax.broadcasted_iota(jnp.int32, (TILE, 1), 0) + (j % 3) * TILE < 383
        errors = jnp.where(keepers, base[j] + op_recv[j].astype(jnp.float32), 0.0).astype(
            jnp.bfloat16
        )
        for side in (1, 0):
            grad = lax.dot_general(
                errors, down[side], (((1,), (1,)), ((), ())), preferred_element_type=jnp.float32
            )
            grad = (grad * slope[j, :, side * 512 : side * 512 + 512]).astype(jnp.bfloat16)
            if side == 1:
                pg_send[j] = grad
                pg_copy(j).start()
            else:
                pg_own[j] = grad

    def arrive(j):
        pg_copy(j).wait_recv()
        flip_copy(j).wait_recv()

    def product(j, k):
        rows = pl.ds(pl.multiple_of(k * CHUNK, CHUNK), CHUNK)
        left = jnp.concatenate([flip[j, rows, :], flip_sib[j, rows, :]], axis=1)
        right = jnp.concatenate([pg_own[j], pg_sib[j]], axis=0)
        return jnp.dot(left, right, preferred_element_type=jnp.float32)

    def gather(j):
        arrive(j)

        def one(k, _):
            rows = pl.ds(pl.multiple_of(k * CHUNK, CHUNK), CHUNK)
            acc[rows, :] += product(j, k)
            return 0

        lax.fori_loop(0, 4, one, 0)

    backward(3)

    def steps(i, _):
        backward((i + 3) % 6)
        gather((i + 2) % 6)
        return 0

    lax.fori_loop(1, 6, steps, 0)

    def z_copy(side, k):
        rows = pl.ds(k * CHUNK, CHUNK)
        return remote(
            fresh.at[rows],
            near.at[side, rows],
            z_s.at[side, k],
            z_r.at[side, k],
            ("up", "down")[side],
        )

    arrive(2)
    for k in range(4):
        rows = slice(k * CHUNK, (k + 1) * CHUNK)
        total = acc[rows, :] + product(2, k)
        fresh[rows, :] = (rest[rows, :] - (drift_stride * factor) * total).astype(jnp.bfloat16)
        z_copy(0, k).start()
        z_copy(1, k).start()

    taken = jnp.full((1, 512), mask[0], jnp.int32) == 1
    mates = jnp.full((1, 512), mate[0], jnp.int32)
    from_below = taken & (mates == rank - 1)
    from_above = taken & (mates == rank + 1)
    lower = jnp.zeros((1, 512), jnp.float32)
    upper = jnp.zeros((1, 512), jnp.float32)
    for k in range(4):
        rows = slice(k * CHUNK, (k + 1) * CHUNK)
        z_copy(0, k).wait_recv()
        z_copy(1, k).wait_recv()
        own = fresh[rows, :].astype(jnp.float32)
        below = near[0, rows, :].astype(jnp.float32)
        above = near[1, rows, :].astype(jnp.float32)
        lower += jnp.sum((own - below) * (own - below), axis=0, keepdims=True)
        upper += jnp.sum((own - above) * (own - above), axis=0, keepdims=True)
        out_ref[0, rows, :] = jnp.where(
            from_below, below, jnp.where(from_above, above, own)
        ).astype(jnp.bfloat16)
    gap_ref[0, 0:1, :] = lower * (1.0 / 1024.0)
    gap_ref[0, 1:2, :] = upper * (1.0 / 1024.0)

    quart.wait_send()
    swap_par.wait_send()
    swap_down.wait_send()
    for copy in spreads:
        copy.wait_send()

    def finish(j, _):
        flip_copy(j).wait_send()
        op_copy(j).wait_send()
        pg_copy(j).wait_send()
        return 0

    lax.fori_loop(0, 6, finish, 0)
    for k in range(4):
        z_copy(0, k).wait_send()
        z_copy(1, k).wait_send()


def body(residual_flow, params, noise, down, heat, mate, mask):
    any_spec = pl.BlockSpec(memory_space=pl.ANY)
    scalar = pl.BlockSpec(memory_space=pltpu.SMEM)
    vmem = pl.BlockSpec(memory_space=pltpu.VMEM)
    bf16, f32 = jnp.bfloat16, jnp.float32
    dma = pltpu.SemaphoreType.DMA
    return pl.pallas_call(
        kernel,
        out_shape=(
            jax.ShapeDtypeStruct((1, 1024, 512), bf16),
            jax.ShapeDtypeStruct((1, 2, 512), f32),
        ),
        in_specs=[any_spec] * 4 + [scalar] * 3,
        out_specs=(vmem, vmem),
        scratch_shapes=[
            pltpu.VMEM((2, 384, 1024), bf16),
            pltpu.VMEM((2, 1024, 512), bf16),
            pltpu.VMEM((1024, 512), bf16),
            pltpu.VMEM((2, 512, 1024), bf16),
            pltpu.VMEM((6, TILE, 1024), bf16),
            pltpu.VMEM((6, 1024, TILE), bf16),
            pltpu.VMEM((6, 1024, TILE), bf16),
            pltpu.VMEM((6, TILE, 1024), f32),
            pltpu.VMEM((6, TILE, 1024), f32),
            pltpu.VMEM((6, TILE, 1024), bf16),
            pltpu.VMEM((6, TILE, 1024), bf16),
            pltpu.VMEM((TILE, 1024), bf16),
            pltpu.VMEM((6, TILE, 512), bf16),
            pltpu.VMEM((6, TILE, 512), bf16),
            pltpu.VMEM((6, TILE, 512), bf16),
            pltpu.VMEM((1024, 512), f32),
            pltpu.VMEM((1024, 512), f32),
            pltpu.VMEM((1024, 512), bf16),
            pltpu.VMEM((2, 1024, 512), bf16),
            dma((4,)),
            dma((2,)),
            dma((2,)),
            dma(()),
            dma(()),
            dma((3,)),
            dma((3,)),
            dma((6,)),
            dma((6,)),
            dma((6,)),
            dma((6,)),
            dma((6,)),
            dma((6,)),
            dma((2, 4)),
            dma((2, 4)),
        ],
        compiler_params=pltpu.CompilerParams(
            collective_id=0, has_side_effects=True, vmem_limit_bytes=56 << 20
        ),
        name="langevin_step",
    )(residual_flow, params, noise, down, heat, mate, mask)


def solution(mesh):
    placed = (
        P("dp", None),
        P("rep", None, "dp"),
        P("rep", None, "dp"),
        P("dp", None),
        P("rep"),
        P("rep"),
        P("rep"),
    )
    return jax.shard_map(
        body,
        mesh=mesh,
        in_specs=placed,
        out_specs=(P("rep", None, "dp"), P("rep", None, "dp")),
        check_vma=False,
    )
```

time: 222 us -> 91.6 us (0.41)
  waiting for transfers between devices: 165 us -> 0 us
  Pallas kernels: 0 us -> 86 us
  matrix products: 16.8 us -> 0 us
  between operations: 15.8 us -> 2.58 us
  other arithmetic: 10.5 us -> 0 us
  starting transfers between devices: 9.85 us -> 0 us
    all_gather x2 -> x0, waiting for transfers between devices: 86 us -> none  [the longest x1 46.1 us: body(): normed = lax.all_gather(normalize(residual_flow), 'dp', axis=0, tiled=True)]
    pallas_call x0 -> x1, Pallas kernels: none -> 86 us  [body(): pl.pallas_call(kernel, out_shape=(jax.ShapeDtypeStruct((1, 1024, 512), bf...]
    reduce_scatter x1 -> x0, waiting for transfers between devices: 58.3 us -> none  [body(): lax.psum_scatter(part.astype(jnp.bfloat16), 'dp', scatter_dimension=0, ti...]
    ppermute x2 -> x0, waiting for transfers between devices: 20.9 us -> none  [shifted(): return lax.ppermute(value, axis, pairs)]
    dot_general x3 -> x0, matrix products: 16.8 us -> none  [the longest x1 9.2 us: body(): lax.dot_general(normed, preact_grad, (((0,), (0,)), ((), ())), preferred_...]
    ppermute x2 -> x0, starting transfers between devices: 9.73 us -> none  [shifted(): return lax.ppermute(value, axis, pairs)]
    reduce_sum x3 -> x0, other arithmetic: 4.78 us -> none  [the longest x1 1.85 us: body(): jnp.mean(lower_diff * lower_diff, axis=0)]
    convert_element_type x2 -> x0, other arithmetic: 2.43 us -> none  [the longest x1 2.27 us: normalize(): return (center * lax.rsqrt(spread + 1e-05)).astype(jnp.bfloat16)]
  transfers between devices with their start and end apart: 5 -> 0, of which waited for: 5 -> 0; matrix products, arithmetic and copies ran while one was open for 0% -> 0% of each run, Pallas kernels for 0% -> 0%
where the time goes in v2:
time: 91.6 us; the launch traced here: 91.4 us
  Pallas kernels  86 us (94%)
  local copies, waits for them, and re-layouts  2.86 us (3%)
  between operations  2.58 us (3%)
    pallas_call x1, Pallas kernels, body(): pl.pallas_call(kernel, out_shape=(jax.ShapeDtypeStruct((1, 1024, 512), bf...  86 us
    unnamed x4, local copies, waits for them, and re-layouts  2.86 us

profile of v2, /device:TPU:1, one launch (start us, length us, event | category | flops | bytes accessed | tf_op | source)
XLA Modules:
  0.0 91.4 jit_solution(8638470384312457847)
XLA Ops:
  2.6 86.0 %langevin_step.1 = (bf16[1,1024,512]{2,1,0:T(8,128)(2,1)}, f32[1,2,512]{2,1,0:T(2,128)}) custom-call(bf16[384,1024]{1,0:T(8,128)(2,1)} %res_hbm.1, bf16[1,1024,512]{2,1,0:T(8,128)(2,1)} %par_hbm.1, bf16[1,1024,512]{2,1,0:T(8,128)(2,1)} %noise_hbm.1, bf16[512,1024]{1,0:T(8,128)(2,1)} %down_hbm.1, f32[1]{0:T(128)S(6)} %copy.11.heat, s32[1]{0:T(128)S(6)} %copy.12.mate, ...), custom_call_target="tpu_custom_call" | custom-call | tf_op jit(solution)/shard_map/langevin_step/pallas_call | solution.py:331
  88.5 0.0 copy-start
  88.5 2.3 %copy.14 = bf16[1,1024,512]{2,1,0:T(8,128)(2,1)} copy(bf16[1,1024,512]{2,1,0:T(8,128)(2,1)} %get-tuple-element.4) | data formatting | bytes 2097152
  90.8 0.0 copy-done
  90.8 0.6 copy.15
Async XLA Ops:
  88.5 2.3 %copy-start = (f32[1,2,512]{2,1,0:T(2,128)S(1)}, f32[1,2,512]{2,1,0:T(2,128)}, u32[]{:S(2)}) copy-start(f32[1,2,512]{2,1,0:T(2,128)} %get-tuple-element.5) | copy-start | bytes 12292

commit v3 on v2

--- a/solution.py
+++ b/solution.py
@@ -12,6 +12,8 @@
 drift_stride = 0.5
 TILE = 128
 CHUNK = 256
+SHARE = 256
+KEEP = 512 - SHARE
 
 
 def place():
@@ -61,13 +63,22 @@
     op_send,
     op_recv,
     hid,
-    pg_send,
-    pg_own,
-    pg_sib,
+    pg_send_b,
+    pg_send_a,
+    pg_b,
+    pg_a,
     acc,
     rest,
-    fresh,
-    near,
+    fresh_b,
+    fresh_a,
+    near_b,
+    near_a,
+    rest_send,
+    rest_near,
+    pg_near,
+    acc_near,
+    gap_sum,
+    gap_recv,
     load_sem,
     swap_s,
     swap_r,
@@ -81,13 +92,25 @@
     op_r,
     pg_s,
     pg_r,
-    z_s,
-    z_r,
+    w_s,
+    w_r,
+    zp_s,
+    zp_r,
+    za_s,
+    za_r,
+    zb_s,
+    zb_r,
+    gx_s,
+    gx_r,
 ):
     factor = 1024 ** (-0.5)
     coeff = math.sqrt(2.0 / math.pi)
     rank, x = place()[:2]
     peer = peers()
+    spot = rank % 4
+    mixes = (spot != 0, spot != 3)
+    sends = (spot != 3, spot != 0)
+    ways = ("up", "down")
 
     def remote(src, dst, send, recv, who):
         return pltpu.make_async_remote_copy(
@@ -132,8 +155,40 @@
             op_send.at[j], op_recv.at[(j + 3) % 6], op_s.at[j], op_r.at[(j + 3) % 6], "partner"
         )
 
-    def pg_copy(j):
-        return remote(pg_send.at[j], pg_sib.at[j], pg_s.at[j], pg_r.at[j], "sibling")
+    def pg_copies(j):
+        low = pl.ds(TILE, TILE)
+        return [
+            remote(pg_send_b.at[j], pg_b.at[j, low], pg_s.at[0, j], pg_r.at[0, j], "sibling"),
+            remote(pg_send_a.at[j], pg_a.at[j, low], pg_s.at[1, j], pg_r.at[1, j], "sibling"),
+        ]
+
+    def w_copy(side):
+        return remote(rest_send, rest_near.at[side], w_s.at[side], w_r.at[side], ways[side])
+
+    def zp_copy(side, j):
+        return remote(
+            pg_b.at[j], pg_near.at[side, j], zp_s.at[side, j], zp_r.at[side, j], ways[side]
+        )
+
+    def za_copy(side, k):
+        rows = pl.ds(k * CHUNK, CHUNK)
+        return remote(
+            fresh_a.at[rows], near_a.at[side, rows], za_s.at[side, k], za_r.at[side, k], ways[side]
+        )
+
+    def zb_copy(side, k):
+        rows = pl.ds(k * CHUNK, CHUNK)
+        return remote(
+            fresh_b.at[rows], near_b.at[side, rows], zb_s.at[side, k], zb_r.at[side, k], ways[side]
+        )
+
+    def gx_copy(side):
+        return remote(
+            gap_sum.at[1 - side], gap_recv.at[side], gx_s.at[side], gx_r.at[side], ways[side]
+        )
+
+    def halves(side, k):
+        return (k < 2) == (side == 0)
 
     def prepare(seq):
         def one(k, _):
@@ -182,10 +237,29 @@
         flip_copy(j).start()
         return 0
 
+    loads[3].wait()
+    heat_root = jnp.sqrt(jnp.full((1, 512), 2.0 * drift_stride * heat[0], jnp.float32))
+
+    def keep(k, _):
+        rows = pl.ds(pl.multiple_of(k * TILE, TILE), TILE)
+        current = par[0, rows, :].astype(jnp.float32)
+        still = current - drift_stride * current + heat_root * noise[rows, :].astype(jnp.float32)
+        rest[rows, :] = still
+        rest_send[rows, :] = still[:, :SHARE].astype(jnp.bfloat16)
+        acc[rows, :] = jnp.zeros((TILE, 512), jnp.float32)
+        for side in range(2):
+            acc_near[side, rows, :] = jnp.zeros((TILE, SHARE), jnp.float32)
+        return 0
+
     prepare(0)
+    lax.fori_loop(0, 8, keep, 0)
+    for side in range(2):
+        pl.when(sends[side])(w_copy(side).start)
     step_ahead(0)
+    lax.fori_loop(0, 3, turn, 0)
     swap_par.wait_recv()
     swap_down.wait_recv()
+    forward(0, 0)
     quart.wait_recv()
     spreads = [
         remote(
@@ -195,22 +269,7 @@
     ]
     for copy in spreads:
         copy.start()
-    lax.fori_loop(0, 3, forward, 0)
-    lax.fori_loop(0, 3, turn, 0)
-
-    loads[3].wait()
-    heat_root = jnp.sqrt(jnp.full((1, 512), 2.0 * drift_stride * heat[0], jnp.float32))
-
-    def keep(k, _):
-        rows = pl.ds(pl.multiple_of(k * TILE, TILE), TILE)
-        current = par[0, rows, :].astype(jnp.float32)
-        rest[rows, :] = (
-            current - drift_stride * current + heat_root * noise[rows, :].astype(jnp.float32)
-        )
-        acc[rows, :] = jnp.zeros((TILE, 512), jnp.float32)
-        return 0
-
-    lax.fori_loop(0, 8, keep, 0)
+    lax.fori_loop(1, 3, forward, 0)
 
     for copy in spreads:
         copy.wait_recv()
@@ -231,20 +290,44 @@
             )
             grad = (grad * slope[j, :, side * 512 : side * 512 + 512]).astype(jnp.bfloat16)
             if side == 1:
-                pg_send[j] = grad
-                pg_copy(j).start()
+                pg_send_b[j] = grad[:, :SHARE]
+                pg_send_a[j] = grad[:, SHARE:]
+                for copy in pg_copies(j):
+                    copy.start()
             else:
-                pg_own[j] = grad
+                pg_b[j, :TILE] = grad[:, :SHARE]
+                pg_a[j, :TILE] = grad[:, SHARE:]
 
     def arrive(j):
-        pg_copy(j).wait_recv()
+        for copy in pg_copies(j):
+            copy.wait_recv()
+        for side in range(2):
+            pl.when(sends[side])(zp_copy(side, j).start)
         flip_copy(j).wait_recv()
 
+    def left(j, k):
+        rows = pl.ds(pl.multiple_of(k * CHUNK, CHUNK), CHUNK)
+        return jnp.concatenate([flip[j, rows, :], flip_sib[j, rows, :]], axis=1)
+
     def product(j, k):
-        rows = pl.ds(pl.multiple_of(k * CHUNK, CHUNK), CHUNK)
-        left = jnp.concatenate([flip[j, rows, :], flip_sib[j, rows, :]], axis=1)
-        right = jnp.concatenate([pg_own[j], pg_sib[j]], axis=0)
-        return jnp.dot(left, right, preferred_element_type=jnp.float32)
+        right = jnp.concatenate([pg_b[j], pg_a[j]], axis=1)
+        return jnp.dot(left(j, k), right, preferred_element_type=jnp.float32)
+
+    def gather_near(j):
+        for side in range(2):
+
+            @pl.when(mixes[side])
+            def _():
+                zp_copy(side, j).wait_recv()
+
+                def one(k, _):
+                    rows = pl.ds(pl.multiple_of(k * CHUNK, CHUNK), CHUNK)
+                    acc_near[side, rows, :] += jnp.dot(
+                        left(j, k), pg_near[side, j], preferred_element_type=jnp.float32
+                    )
+                    return 0
+
+                lax.fori_loop(0, 4, one, 0)
 
     def gather(j):
         arrive(j)
@@ -257,52 +340,108 @@
         lax.fori_loop(0, 4, one, 0)
 
     backward(3)
+    backward(4)
+    gather(3)
 
     def steps(i, _):
         backward((i + 3) % 6)
         gather((i + 2) % 6)
+        gather_near((i + 1) % 6)
         return 0
 
-    lax.fori_loop(1, 6, steps, 0)
-
-    def z_copy(side, k):
-        rows = pl.ds(k * CHUNK, CHUNK)
-        return remote(
-            fresh.at[rows],
-            near.at[side, rows],
-            z_s.at[side, k],
-            z_r.at[side, k],
-            ("up", "down")[side],
-        )
+    lax.fori_loop(2, 6, steps, 0)
 
     arrive(2)
     for k in range(4):
         rows = slice(k * CHUNK, (k + 1) * CHUNK)
         total = acc[rows, :] + product(2, k)
-        fresh[rows, :] = (rest[rows, :] - (drift_stride * factor) * total).astype(jnp.bfloat16)
-        z_copy(0, k).start()
-        z_copy(1, k).start()
+        moved = (rest[rows, :] - (drift_stride * factor) * total).astype(jnp.bfloat16)
+        fresh_b[rows, :] = moved[:, :SHARE]
+        fresh_a[rows, :] = moved[:, SHARE:]
+        for side in range(2):
+            pl.when(sends[side])(za_copy(side, k).start)
+            if halves(side, k):
+
+                @pl.when(jnp.logical_not(sends[side]))
+                def _():
+                    za_copy(side, k).start()
+                    zb_copy(side, k).start()
+
+    gather_near(1)
+    gather_near(2)
+    for side in range(2):
+
+        @pl.when(mixes[side])
+        def _():
+            w_copy(side).wait_recv()
+
+            def one(k, _):
+                rows = pl.ds(pl.multiple_of(k * CHUNK, CHUNK), CHUNK)
+                near_b[side, rows, :] = (
+                    rest_near[side, rows, :].astype(jnp.float32)
+                    - (drift_stride * factor) * acc_near[side, rows, :]
+                ).astype(jnp.bfloat16)
+                return 0
+
+            lax.fori_loop(0, 4, one, 0)
 
     taken = jnp.full((1, 512), mask[0], jnp.int32) == 1
     mates = jnp.full((1, 512), mate[0], jnp.int32)
-    from_below = taken & (mates == rank - 1)
-    from_above = taken & (mates == rank + 1)
-    lower = jnp.zeros((1, 512), jnp.float32)
-    upper = jnp.zeros((1, 512), jnp.float32)
+    picks = (taken & (mates == rank - 1), taken & (mates == rank + 1))
+    gap_sum[...] = jnp.zeros((2, 8, 512), jnp.float32)
+    pairs = ((0, SHARE, fresh_b, near_b), (SHARE, 512, fresh_a, near_a))
     for k in range(4):
         rows = slice(k * CHUNK, (k + 1) * CHUNK)
-        z_copy(0, k).wait_recv()
-        z_copy(1, k).wait_recv()
-        own = fresh[rows, :].astype(jnp.float32)
-        below = near[0, rows, :].astype(jnp.float32)
-        above = near[1, rows, :].astype(jnp.float32)
-        lower += jnp.sum((own - below) * (own - below), axis=0, keepdims=True)
-        upper += jnp.sum((own - above) * (own - above), axis=0, keepdims=True)
-        out_ref[0, rows, :] = jnp.where(
-            from_below, below, jnp.where(from_above, above, own)
-        ).astype(jnp.bfloat16)
-    gap_ref[0, 0:1, :] = lower * (1.0 / 1024.0)
-    gap_ref[0, 1:2, :] = upper * (1.0 / 1024.0)
+
+        def add_gap(side):
+            for first, last, own_ref, near_ref in pairs:
+                gap = own_ref[rows, :].astype(jnp.float32) - near_ref[side, rows, :].astype(
+                    jnp.float32
+                )
+                gap_sum[side, :, first:last] += jnp.sum(
+                    (gap * gap).reshape(CHUNK // 8, 8, last - first), axis=0
+                )
+
+        for side in range(2):
+
+            @pl.when(mixes[side])
+            def _():
+                za_copy(side, k).wait_recv()
+                add_gap(side)
+
+            if halves(side, k):
+
+                @pl.when(jnp.logical_not(mixes[side]))
+                def _():
+                    za_copy(side, k).wait_recv()
+                    zb_copy(side, k).wait_recv()
+                    add_gap(side)
+
+        for side in range(2):
+            if k == (1, 3)[side]:
+                pl.when(jnp.logical_not(mixes[side]))(gx_copy(1 - side).start)
+        for first, last, own_ref, near_ref in pairs:
+            out_ref[0, rows, first:last] = jnp.where(
+                picks[0][:, first:last],
+                near_ref[0, rows, :],
+                jnp.where(picks[1][:, first:last], near_ref[1, rows, :], own_ref[rows, :]),
+            )
+
+    for side in range(2):
+
+        @pl.when(jnp.logical_not(mixes[side]))
+        def _():
+            gx_copy(side).wait_recv()
+            gap_recv[side] += gap_sum[side]
+            gap_ref[0, side : side + 1, :] = jnp.sum(gap_recv[side], axis=0, keepdims=True) * (
+                1.0 / 1024.0
+            )
+
+        @pl.when(mixes[side])
+        def _():
+            gap_ref[0, side : side + 1, :] = jnp.sum(gap_sum[side], axis=0, keepdims=True) * (
+                1.0 / 1024.0
+            )
 
     quart.wait_send()
     swap_par.wait_send()
@@ -313,13 +452,28 @@
     def finish(j, _):
         flip_copy(j).wait_send()
         op_copy(j).wait_send()
-        pg_copy(j).wait_send()
+        for copy in pg_copies(j):
+            copy.wait_send()
+        for side in range(2):
+            pl.when(sends[side])(zp_copy(side, j).wait_send)
         return 0
 
     lax.fori_loop(0, 6, finish, 0)
-    for k in range(4):
-        z_copy(0, k).wait_send()
-        z_copy(1, k).wait_send()
+    for side in range(2):
+
+        @pl.when(sends[side])
+        def _():
+            w_copy(side).wait_send()
+            for k in range(4):
+                za_copy(side, k).wait_send()
+
+        @pl.when(jnp.logical_not(sends[side]))
+        def _():
+            gx_copy(side).wait_send()
+            for k in range(4):
+                if halves(side, k):
+                    za_copy(side, k).wait_send()
+                    zb_copy(side, k).wait_send()
 
 
 def body(residual_flow, params, noise, down, heat, mate, mask):
@@ -349,13 +503,22 @@
             pltpu.VMEM((6, TILE, 1024), bf16),
             pltpu.VMEM((6, TILE, 1024), bf16),
             pltpu.VMEM((TILE, 1024), bf16),
-            pltpu.VMEM((6, TILE, 512), bf16),
-            pltpu.VMEM((6, TILE, 512), bf16),
-            pltpu.VMEM((6, TILE, 512), bf16),
+            pltpu.VMEM((6, TILE, SHARE), bf16),
+            pltpu.VMEM((6, TILE, KEEP), bf16),
+            pltpu.VMEM((6, 2 * TILE, SHARE), bf16),
+            pltpu.VMEM((6, 2 * TILE, KEEP), bf16),
             pltpu.VMEM((1024, 512), f32),
             pltpu.VMEM((1024, 512), f32),
-            pltpu.VMEM((1024, 512), bf16),
-            pltpu.VMEM((2, 1024, 512), bf16),
+            pltpu.VMEM((1024, SHARE), bf16),
+            pltpu.VMEM((1024, KEEP), bf16),
+            pltpu.VMEM((2, 1024, SHARE), bf16),
+            pltpu.VMEM((2, 1024, KEEP), bf16),
+            pltpu.VMEM((1024, SHARE), bf16),
+            pltpu.VMEM((2, 1024, SHARE), bf16),
+            pltpu.VMEM((2, 6, 2 * TILE, SHARE), bf16),
+            pltpu.VMEM((2, 1024, SHARE), f32),
+            pltpu.VMEM((2, 8, 512), f32),
+            pltpu.VMEM((2, 8, 512), f32),
             dma((4,)),
             dma((2,)),
             dma((2,)),
@@ -367,10 +530,18 @@
             dma((6,)),
             dma((6,)),
             dma((6,)),
-            dma((6,)),
-            dma((6,)),
+            dma((2, 6)),
+            dma((2, 6)),
+            dma((2,)),
+            dma((2,)),
+            dma((2, 6)),
+            dma((2, 6)),
             dma((2, 4)),
             dma((2, 4)),
+            dma((2, 4)),
+            dma((2, 4)),
+            dma((2,)),
+            dma((2,)),
         ],
         compiler_params=pltpu.CompilerParams(
             collective_id=0, has_side_effects=True, vmem_limit_bytes=56 << 20

time: 91.6 us -> 86.9 us (0.949)
  Pallas kernels: 86 us -> 81.2 us
    pallas_call x1, Pallas kernels: 86 us -> 81.2 us  [body(): pl.pallas_call(kernel, out_shape=(jax.ShapeDtypeStruct((1, 1024, 512), bf...]
where the time goes in v3:
time: 86.9 us; the launch traced here: 86.7 us
  Pallas kernels  81.2 us (93%)
  local copies, waits for them, and re-layouts  2.86 us (3%)
  between operations  2.58 us (3%)
    pallas_call x1, Pallas kernels, body(): pl.pallas_call(kernel, out_shape=(jax.ShapeDtypeStruct((1, 1024, 512), bf...  81.2 us
    unnamed x4, local copies, waits for them, and re-layouts  2.86 us

profile of v3, /device:TPU:1, one launch (start us, length us, event | category | flops | bytes accessed | tf_op | source)
XLA Modules:
  0.0 86.7 jit_solution(1771530653491293839)
XLA Ops:
  2.6 81.2 %langevin_step.1 = (bf16[1,1024,512]{2,1,0:T(8,128)(2,1)}, f32[1,2,512]{2,1,0:T(2,128)}) custom-call(bf16[384,1024]{1,0:T(8,128)(2,1)} %res_hbm.1, bf16[1,1024,512]{2,1,0:T(8,128)(2,1)} %par_hbm.1, bf16[1,1024,512]{2,1,0:T(8,128)(2,1)} %noise_hbm.1, bf16[512,1024]{1,0:T(8,128)(2,1)} %down_hbm.1, f32[1]{0:T(128)S(6)} %copy.11.heat, s32[1]{0:T(128)S(6)} %copy.12.mate, ...), custom_call_target="tpu_custom_call" | custom-call | tf_op jit(solution)/shard_map/langevin_step/pallas_call | solution.py:485
  83.8 0.0 copy-start
  83.8 2.3 %copy.14 = bf16[1,1024,512]{2,1,0:T(8,128)(2,1)} copy(bf16[1,1024,512]{2,1,0:T(8,128)(2,1)} %get-tuple-element.4) | data formatting | bytes 2097152
  86.1 0.0 copy-done
  86.1 0.6 copy.15
Async XLA Ops:
  83.8 2.3 %copy-start = (f32[1,2,512]{2,1,0:T(2,128)S(1)}, f32[1,2,512]{2,1,0:T(2,128)}, u32[]{:S(2)}) copy-start(f32[1,2,512]{2,1,0:T(2,128)} %get-tuple-element.5) | copy-start | bytes 12292

commit v4 on v3

--- a/solution.py
+++ b/solution.py
@@ -111,6 +111,7 @@
     mixes = (spot != 0, spot != 3)
     sends = (spot != 3, spot != 0)
     ways = ("up", "down")
+    turned = 2 - 2 * ((spot + 3) // 4)
 
     def remote(src, dst, send, recv, who):
         return pltpu.make_async_remote_copy(
@@ -170,14 +171,17 @@
             pg_b.at[j], pg_near.at[side, j], zp_s.at[side, j], zp_r.at[side, j], ways[side]
         )
 
+    def chunk(k):
+        return pl.ds(pl.multiple_of(k * CHUNK, CHUNK), CHUNK)
+
     def za_copy(side, k):
-        rows = pl.ds(k * CHUNK, CHUNK)
+        rows = chunk(k)
         return remote(
             fresh_a.at[rows], near_a.at[side, rows], za_s.at[side, k], za_r.at[side, k], ways[side]
         )
 
     def zb_copy(side, k):
-        rows = pl.ds(k * CHUNK, CHUNK)
+        rows = chunk(k)
         return remote(
             fresh_b.at[rows], near_b.at[side, rows], zb_s.at[side, k], zb_r.at[side, k], ways[side]
         )
@@ -186,9 +190,6 @@
         return remote(
             gap_sum.at[1 - side], gap_recv.at[side], gx_s.at[side], gx_r.at[side], ways[side]
         )
-
-    def halves(side, k):
-        return (k < 2) == (side == 0)
 
     def prepare(seq):
         def one(k, _):
@@ -209,12 +210,12 @@
             for k in range(3):
                 base[seq * 3 + k, :, cols] = ahead[k * TILE : (k + 1) * TILE]
 
-    def forward(j, _):
+    def forward_in(j, side):
         rows = nrm[j]
-        for c in range(4):
-            cols = slice((c % 2) * CHUNK, (c % 2 + 1) * CHUNK)
-            wide = slice(c * CHUNK, (c + 1) * CHUNK)
-            v = jnp.dot(rows, par[c // 2, :, cols], preferred_element_type=jnp.float32) * factor
+        for c in range(2):
+            cols = slice(c * CHUNK, (c + 1) * CHUNK)
+            wide = slice(side * 512 + c * CHUNK, side * 512 + (c + 1) * CHUNK)
+            v = jnp.dot(rows, par[side, :, cols], preferred_element_type=jnp.float32) * factor
             square = v * v
             tangent = jnp.tanh(coeff * v * (1.0 + 0.044715 * square))
             half = 0.5 * (1.0 + tangent)
@@ -222,6 +223,8 @@
             slope[j, :, wide] = half + 0.5 * coeff * v * (1.0 - tangent * tangent) * (
                 1.0 + 3.0 * 0.044715 * square
             )
+
+    def forward_out(j):
         for c in range(4):
             wide = slice(c * CHUNK, (c + 1) * CHUNK)
             part = jnp.dot(
@@ -230,6 +233,11 @@
             base[j, :, wide] += part
             op_send[j, :, wide] = part.astype(jnp.bfloat16)
         op_copy(j).start()
+
+    def forward(j, _):
+        forward_in(j, 0)
+        forward_in(j, 1)
+        forward_out(j)
         return 0
 
     def turn(j, _):
@@ -246,20 +254,18 @@
         still = current - drift_stride * current + heat_root * noise[rows, :].astype(jnp.float32)
         rest[rows, :] = still
         rest_send[rows, :] = still[:, :SHARE].astype(jnp.bfloat16)
-        acc[rows, :] = jnp.zeros((TILE, 512), jnp.float32)
-        for side in range(2):
-            acc_near[side, rows, :] = jnp.zeros((TILE, SHARE), jnp.float32)
         return 0
 
     prepare(0)
+    step_ahead(0)
+    forward_in(0, 0)
     lax.fori_loop(0, 8, keep, 0)
     for side in range(2):
         pl.when(sends[side])(w_copy(side).start)
-    step_ahead(0)
-    lax.fori_loop(0, 3, turn, 0)
     swap_par.wait_recv()
+    forward_in(0, 1)
     swap_down.wait_recv()
-    forward(0, 0)
+    forward_out(0)
     quart.wait_recv()
     spreads = [
         remote(
@@ -270,6 +276,7 @@
     for copy in spreads:
         copy.start()
     lax.fori_loop(1, 3, forward, 0)
+    lax.fori_loop(0, 3, turn, 0)
 
     for copy in spreads:
         copy.wait_recv()
@@ -305,127 +312,135 @@
             pl.when(sends[side])(zp_copy(side, j).start)
         flip_copy(j).wait_recv()
 
-    def left(j, k):
-        rows = pl.ds(pl.multiple_of(k * CHUNK, CHUNK), CHUNK)
-        return jnp.concatenate([flip[j, rows, :], flip_sib[j, rows, :]], axis=1)
-
-    def product(j, k):
-        right = jnp.concatenate([pg_b[j], pg_a[j]], axis=1)
-        return jnp.dot(left(j, k), right, preferred_element_type=jnp.float32)
-
-    def gather_near(j):
+    def joined(tiles, rows):
+        pieces = []
+        for j in tiles:
+            pieces += [flip[j, rows, :], flip_sib[j, rows, :]]
+        return jnp.concatenate(pieces, axis=1)
+
+    def product(tiles, k):
+        right = jnp.concatenate(
+            [
+                pg_b[tiles[0] : tiles[-1] + 1].reshape(2 * TILE * len(tiles), SHARE),
+                pg_a[tiles[0] : tiles[-1] + 1].reshape(2 * TILE * len(tiles), KEEP),
+            ],
+            axis=1,
+        )
+        return jnp.dot(joined(tiles, chunk(k)), right, preferred_element_type=jnp.float32)
+
+    def gather_near(tiles, fresh_start):
         for side in range(2):
 
             @pl.when(mixes[side])
             def _():
-                zp_copy(side, j).wait_recv()
+                for j in tiles:
+                    zp_copy(side, j).wait_recv()
 
                 def one(k, _):
-                    rows = pl.ds(pl.multiple_of(k * CHUNK, CHUNK), CHUNK)
-                    acc_near[side, rows, :] += jnp.dot(
-                        left(j, k), pg_near[side, j], preferred_element_type=jnp.float32
+                    right = pg_near[side, tiles[0] : tiles[-1] + 1].reshape(
+                        2 * TILE * len(tiles), SHARE
                     )
+                    more = jnp.dot(
+                        joined(tiles, chunk(k)), right, preferred_element_type=jnp.float32
+                    )
+                    if fresh_start:
+                        acc_near[side, chunk(k), :] = more
+                    else:
+                        near_b[side, chunk(k), :] = (
+                            rest_near[side, chunk(k), :].astype(jnp.float32)
+                            - (drift_stride * factor) * (acc_near[side, chunk(k), :] + more)
+                        ).astype(jnp.bfloat16)
                     return 0
 
+                if not fresh_start:
+                    w_copy(side).wait_recv()
                 lax.fori_loop(0, 4, one, 0)
 
-    def gather(j):
-        arrive(j)
-
-        def one(k, _):
-            rows = pl.ds(pl.multiple_of(k * CHUNK, CHUNK), CHUNK)
-            acc[rows, :] += product(j, k)
-            return 0
-
-        lax.fori_loop(0, 4, one, 0)
+    def first_sum(k, _):
+        acc[chunk(k), :] = product((3, 4, 5), k)
+        return 0
+
+    def second_sum(k, _):
+        acc[chunk(k), :] += product((0, 1), k)
+        return 0
 
     backward(3)
     backward(4)
-    gather(3)
-
-    def steps(i, _):
-        backward((i + 3) % 6)
-        gather((i + 2) % 6)
-        gather_near((i + 1) % 6)
-        return 0
-
-    lax.fori_loop(2, 6, steps, 0)
-
+    arrive(3)
+    backward(5)
+    arrive(4)
+    backward(0)
+    arrive(5)
+    lax.fori_loop(0, 4, first_sum, 0)
+    backward(1)
+    arrive(0)
+    gather_near((3, 4, 5), True)
+    backward(2)
+    arrive(1)
+    lax.fori_loop(0, 4, second_sum, 0)
     arrive(2)
+
     for k in range(4):
-        rows = slice(k * CHUNK, (k + 1) * CHUNK)
-        total = acc[rows, :] + product(2, k)
+        rows = chunk((k + turned) % 4)
+        total = acc[rows, :] + product((2,), (k + turned) % 4)
         moved = (rest[rows, :] - (drift_stride * factor) * total).astype(jnp.bfloat16)
         fresh_b[rows, :] = moved[:, :SHARE]
         fresh_a[rows, :] = moved[:, SHARE:]
         for side in range(2):
-            pl.when(sends[side])(za_copy(side, k).start)
-            if halves(side, k):
+            pl.when(sends[side])(za_copy(side, (k + turned) % 4).start)
+            if k < 2:
 
                 @pl.when(jnp.logical_not(sends[side]))
                 def _():
-                    za_copy(side, k).start()
-                    zb_copy(side, k).start()
-
-    gather_near(1)
-    gather_near(2)
-    for side in range(2):
-
-        @pl.when(mixes[side])
-        def _():
-            w_copy(side).wait_recv()
-
-            def one(k, _):
-                rows = pl.ds(pl.multiple_of(k * CHUNK, CHUNK), CHUNK)
-                near_b[side, rows, :] = (
-                    rest_near[side, rows, :].astype(jnp.float32)
-                    - (drift_stride * factor) * acc_near[side, rows, :]
-                ).astype(jnp.bfloat16)
-                return 0
-
-            lax.fori_loop(0, 4, one, 0)
+                    za_copy(side, (k + turned) % 4).start()
+                    zb_copy(side, (k + turned) % 4).start()
+
+    gather_near((0, 1, 2), False)
 
     taken = jnp.full((1, 512), mask[0], jnp.int32) == 1
     mates = jnp.full((1, 512), mate[0], jnp.int32)
     picks = (taken & (mates == rank - 1), taken & (mates == rank + 1))
     gap_sum[...] = jnp.zeros((2, 8, 512), jnp.float32)
     pairs = ((0, SHARE, fresh_b, near_b), (SHARE, 512, fresh_a, near_a))
-    for k in range(4):
-        rows = slice(k * CHUNK, (k + 1) * CHUNK)
-
-        def add_gap(side):
-            for first, last, own_ref, near_ref in pairs:
-                gap = own_ref[rows, :].astype(jnp.float32) - near_ref[side, rows, :].astype(
-                    jnp.float32
-                )
-                gap_sum[side, :, first:last] += jnp.sum(
-                    (gap * gap).reshape(CHUNK // 8, 8, last - first), axis=0
-                )
-
+
+    def add_gap(side, k):
+        for first, last, own_ref, near_ref in pairs:
+            gap = own_ref[chunk(k), :].astype(jnp.float32) - near_ref[side, chunk(k), :].astype(
+                jnp.float32
+            )
+            gap_sum[side, :, first:last] += jnp.sum(
+                (gap * gap).reshape(CHUNK // 8, 8, last - first), axis=0
+            )
+
+    for side in range(2):
+
+        @pl.when(jnp.logical_not(mixes[side]))
+        def _():
+            for k in (2 * side, 2 * side + 1):
+                za_copy(side, k).wait_recv()
+                zb_copy(side, k).wait_recv()
+                add_gap(side, k)
+            gx_copy(1 - side).start()
+
+    def mix(k, _):
         for side in range(2):
 
             @pl.when(mixes[side])
             def _():
                 za_copy(side, k).wait_recv()
-                add_gap(side)
-
-            if halves(side, k):
-
-                @pl.when(jnp.logical_not(mixes[side]))
-                def _():
-                    za_copy(side, k).wait_recv()
-                    zb_copy(side, k).wait_recv()
-                    add_gap(side)
-
-        for side in range(2):
-            if k == (1, 3)[side]:
-                pl.when(jnp.logical_not(mixes[side]))(gx_copy(1 - side).start)
+                add_gap(side, k)
+
         for first, last, own_ref, near_ref in pairs:
-            out_ref[0, rows, first:last] = jnp.where(
+            out_ref[0, chunk(k), first:last] = jnp.where(
                 picks[0][:, first:last],
-                near_ref[0, rows, :],
-                jnp.where(picks[1][:, first:last], near_ref[1, rows, :], own_ref[rows, :]),
-            )
+                near_ref[0, chunk(k), :],
+                jnp.where(
+                    picks[1][:, first:last], near_ref[1, chunk(k), :], own_ref[chunk(k), :]
+                ),
+            )
+        return 0
+
+    lax.fori_loop(0, 4, mix, 0)
 
     for side in range(2):
 
@@ -470,10 +485,9 @@
         @pl.when(jnp.logical_not(sends[side]))
         def _():
             gx_copy(side).wait_send()
-            for k in range(4):
-                if halves(side, k):
-                    za_copy(side, k).wait_send()
-                    zb_copy(side, k).wait_send()
+            for k in (2 * side, 2 * side + 1):
+                za_copy(side, k).wait_send()
+                zb_copy(side, k).wait_send()
 
 
 def body(residual_flow, params, noise, down, heat, mate, mask):
@@ -544,10 +558,18 @@
             dma((2,)),
         ],
         compiler_params=pltpu.CompilerParams(
-            collective_id=0, has_side_effects=True, vmem_limit_bytes=56 << 20
+            collective_id=0, has_side_effects=True, vmem_limit_bytes=52 << 20
         ),
         name="langevin_step",
-    )(residual_flow, params, noise, down, heat, mate, mask)
+    )(
+        *(
+            pltpu.with_memory_space_constraint(each, pltpu.HBM)
+            for each in (residual_flow, params, noise, down)
+        ),
+        heat,
+        mate,
+        mask,
+    )
 
 
 def solution(mesh):

time: 86.9 us -> 83 us (0.955)
  Pallas kernels: 81.2 us -> 78.7 us
  local copies, waits for them, and re-layouts: 2.86 us -> 1.56 us
    pallas_call x1, Pallas kernels: 81.2 us -> 78.7 us  [body(): pl.pallas_call(kernel, out_shape=(jax.ShapeDtypeStruct((1, 1024, 512), bf...]
    unnamed x4 -> x2, local copies, waits for them, and re-layouts: 2.86 us -> 1.56 us
where the time goes in v4:
time: 83 us; the launch traced here: 82.9 us
  Pallas kernels  78.7 us (95%)
  between operations  2.58 us (3%)
  local copies, waits for them, and re-layouts  1.56 us (2%)
    pallas_call x1, Pallas kernels, body(): pl.pallas_call(kernel, out_shape=(jax.ShapeDtypeStruct((1, 1024, 512), bf...  78.7 us

profile of v4, /device:TPU:1, one launch (start us, length us, event | category | flops | bytes accessed | tf_op | source)
XLA Modules:
  0.0 82.9 jit_solution(5556269778441803899)
XLA Ops:
  2.6 78.7 %langevin_step.1 = (bf16[1,1024,512]{2,1,0:T(8,128)(2,1)S(1)}, f32[1,2,512]{2,1,0:T(2,128)S(1)}) custom-call(bf16[384,1024]{1,0:T(8,128)(2,1)} %res_hbm.1, bf16[1,1024,512]{2,1,0:T(8,128)(2,1)} %par_hbm.1, bf16[1,1024,512]{2,1,0:T(8,128)(2,1)} %noise_hbm.1, bf16[512,1024]{1,0:T(8,128)(2,1)} %down_hbm.1, f32[1]{0:T(128)S(6)} %copy.11.heat, s32[1]{0:T(128)S(6)} %copy.12.mate, ...), custom_call_target="tpu_custom_call" | custom-call | tf_op jit(solution)/shard_map/langevin_step/pallas_call | solution.py:499
  81.3 1.0 %copy.14 = bf16[1,1024,512]{2,1,0:T(8,128)(2,1)} copy(bf16[1,1024,512]{2,1,0:T(8,128)(2,1)S(1)} %get-tuple-element.4) | data formatting | bytes 2097152
  82.3 0.6 copy.15

commit v5 on v4

--- a/solution.py
+++ b/solution.py
@@ -14,6 +14,7 @@
 CHUNK = 256
 SHARE = 256
 KEEP = 512 - SHARE
+EDGE = (((0, 256), (256, 448), (448, 576)), ((768, 1024), (576, 768), (448, 576)))
 
 
 def place():
@@ -78,6 +79,7 @@
     pg_near,
     acc_near,
     gap_sum,
+    gap_send,
     gap_recv,
     load_sem,
     swap_s,
@@ -180,15 +182,28 @@
             fresh_a.at[rows], near_a.at[side, rows], za_s.at[side, k], za_r.at[side, k], ways[side]
         )
 
-    def zb_copy(side, k):
-        rows = chunk(k)
-        return remote(
-            fresh_b.at[rows], near_b.at[side, rows], zb_s.at[side, k], zb_r.at[side, k], ways[side]
-        )
+    def edge_copies(side, k):
+        rows = slice(*EDGE[side][k])
+        return [
+            remote(
+                fresh_a.at[rows],
+                near_a.at[side, rows],
+                za_s.at[side, k],
+                za_r.at[side, k],
+                ways[side],
+            ),
+            remote(
+                fresh_b.at[rows],
+                near_b.at[side, rows],
+                zb_s.at[side, k],
+                zb_r.at[side, k],
+                ways[side],
+            ),
+        ]
 
     def gx_copy(side):
         return remote(
-            gap_sum.at[1 - side], gap_recv.at[side], gx_s.at[side], gx_r.at[side], ways[side]
+            gap_send.at[1 - side], gap_recv.at[side], gx_s.at[side], gx_r.at[side], ways[side]
         )
 
     def prepare(seq):
@@ -369,15 +384,15 @@
     arrive(3)
     backward(5)
     arrive(4)
-    backward(0)
     arrive(5)
     lax.fori_loop(0, 4, first_sum, 0)
-    backward(1)
+    backward(0)
     arrive(0)
     gather_near((3, 4, 5), True)
-    backward(2)
+    backward(1)
     arrive(1)
     lax.fori_loop(0, 4, second_sum, 0)
+    backward(2)
     arrive(2)
 
     for k in range(4):
@@ -388,12 +403,13 @@
         fresh_a[rows, :] = moved[:, SHARE:]
         for side in range(2):
             pl.when(sends[side])(za_copy(side, (k + turned) % 4).start)
-            if k < 2:
+            if k in (1, 3):
 
                 @pl.when(jnp.logical_not(sends[side]))
                 def _():
-                    za_copy(side, (k + turned) % 4).start()
-                    zb_copy(side, (k + turned) % 4).start()
+                    for piece in ((0, 1), (2,))[k // 2]:
+                        for copy in edge_copies(side, piece):
+                            copy.start()
 
     gather_near((0, 1, 2), False)
 
@@ -403,23 +419,25 @@
     gap_sum[...] = jnp.zeros((2, 8, 512), jnp.float32)
     pairs = ((0, SHARE, fresh_b, near_b), (SHARE, 512, fresh_a, near_a))
 
-    def add_gap(side, k):
+    def add_gap(side, rows, count):
         for first, last, own_ref, near_ref in pairs:
-            gap = own_ref[chunk(k), :].astype(jnp.float32) - near_ref[side, chunk(k), :].astype(
+            gap = own_ref[rows, :].astype(jnp.float32) - near_ref[side, rows, :].astype(
                 jnp.float32
             )
             gap_sum[side, :, first:last] += jnp.sum(
-                (gap * gap).reshape(CHUNK // 8, 8, last - first), axis=0
+                (gap * gap).reshape(count // 8, 8, last - first), axis=0
             )
 
     for side in range(2):
 
         @pl.when(jnp.logical_not(mixes[side]))
         def _():
-            for k in (2 * side, 2 * side + 1):
-                za_copy(side, k).wait_recv()
-                zb_copy(side, k).wait_recv()
-                add_gap(side, k)
+            for piece in (0, 1):
+                for copy in edge_copies(side, piece):
+                    copy.wait_recv()
+                first, last = EDGE[side][piece]
+                add_gap(side, slice(first, last), last - first)
+            gap_send[side] = gap_sum[side]
             gx_copy(1 - side).start()
 
     def mix(k, _):
@@ -428,16 +446,20 @@
             @pl.when(mixes[side])
             def _():
                 za_copy(side, k).wait_recv()
-                add_gap(side, k)
-
-        for first, last, own_ref, near_ref in pairs:
-            out_ref[0, chunk(k), first:last] = jnp.where(
-                picks[0][:, first:last],
-                near_ref[0, chunk(k), :],
-                jnp.where(
-                    picks[1][:, first:last], near_ref[1, chunk(k), :], own_ref[chunk(k), :]
-                ),
-            )
+                add_gap(side, chunk(k), CHUNK)
+
+        def choose(sides):
+            for first, last, own_ref, near_ref in pairs:
+                value = own_ref[chunk(k), :]
+                for side in sides:
+                    value = jnp.where(
+                        picks[side][:, first:last], near_ref[side, chunk(k), :], value
+                    )
+                out_ref[0, chunk(k), first:last] = value
+
+        pl.when(mixes[0] & mixes[1])(lambda: choose((0, 1)))
+        pl.when(jnp.logical_not(mixes[0]))(lambda: choose((1,)))
+        pl.when(jnp.logical_not(mixes[1]))(lambda: choose((0,)))
         return 0
 
     lax.fori_loop(0, 4, mix, 0)
@@ -446,6 +468,10 @@
 
         @pl.when(jnp.logical_not(mixes[side]))
         def _():
+            for copy in edge_copies(side, 2):
+                copy.wait_recv()
+            first, last = EDGE[side][2]
+            add_gap(side, slice(first, last), last - first)
             gx_copy(side).wait_recv()
             gap_recv[side] += gap_sum[side]
             gap_ref[0, side : side + 1, :] = jnp.sum(gap_recv[side], axis=0, keepdims=True) * (
@@ -485,9 +511,9 @@
         @pl.when(jnp.logical_not(sends[side]))
         def _():
             gx_copy(side).wait_send()
-            for k in (2 * side, 2 * side + 1):
-                za_copy(side, k).wait_send()
-                zb_copy(side, k).wait_send()
+            for piece in range(3):
+                for copy in edge_copies(side, piece):
+                    copy.wait_send()
 
 
 def body(residual_flow, params, noise, down, heat, mate, mask):
@@ -533,6 +559,7 @@
             pltpu.VMEM((2, 1024, SHARE), f32),
             pltpu.VMEM((2, 8, 512), f32),
             pltpu.VMEM((2, 8, 512), f32),
+            pltpu.VMEM((2, 8, 512), f32),
             dma((4,)),
             dma((2,)),
             dma((2,)),

time: 83 us -> 81.6 us (0.983)
  Pallas kernels: 78.7 us -> 77.3 us
    pallas_call x1, Pallas kernels: 78.7 us -> 77.3 us  [body(): pl.pallas_call(kernel, out_shape=(jax.ShapeDtypeStruct((1, 1024, 512), bf...]
where the time goes in v5:
time: 81.6 us; the launch traced here: 81.5 us
  Pallas kernels  77.3 us (95%)
  between operations  2.58 us (3%)
  local copies, waits for them, and re-layouts  1.56 us (2%)
    pallas_call x1, Pallas kernels, body(): pl.pallas_call(kernel, out_shape=(jax.ShapeDtypeStruct((1, 1024, 512), bf...  77.3 us

profile of v5, /device:TPU:1, one launch (start us, length us, event | category | flops | bytes accessed | tf_op | source)
XLA Modules:
  0.0 81.5 jit_solution(14649707231759542044)
XLA Ops:
  2.6 77.3 %langevin_step.1 = (bf16[1,1024,512]{2,1,0:T(8,128)(2,1)S(1)}, f32[1,2,512]{2,1,0:T(2,128)S(1)}) custom-call(bf16[384,1024]{1,0:T(8,128)(2,1)} %res_hbm.1, bf16[1,1024,512]{2,1,0:T(8,128)(2,1)} %par_hbm.1, bf16[1,1024,512]{2,1,0:T(8,128)(2,1)} %noise_hbm.1, bf16[512,1024]{1,0:T(8,128)(2,1)} %down_hbm.1, f32[1]{0:T(128)S(6)} %copy.11.heat, s32[1]{0:T(128)S(6)} %copy.12.mate, ...), custom_call_target="tpu_custom_call" | custom-call | tf_op jit(solution)/shard_map/langevin_step/pallas_call | solution.py:525
  79.9 1.0 %copy.14 = bf16[1,1024,512]{2,1,0:T(8,128)(2,1)} copy(bf16[1,1024,512]{2,1,0:T(8,128)(2,1)S(1)} %get-tuple-element.4) | data formatting | bytes 2097152
  80.9 0.6 copy.15

commit v6 on v5

--- a/solution.py
+++ b/solution.py
@@ -14,7 +14,7 @@
 CHUNK = 256
 SHARE = 256
 KEEP = 512 - SHARE
-EDGE = (((0, 256), (256, 448), (448, 576)), ((768, 1024), (576, 768), (448, 576)))
+EDGE = (((0, 256), (256, 416), (416, 608)), ((768, 1024), (608, 768), (416, 608)))
 
 
 def place():
@@ -403,13 +403,12 @@
         fresh_a[rows, :] = moved[:, SHARE:]
         for side in range(2):
             pl.when(sends[side])(za_copy(side, (k + turned) % 4).start)
-            if k in (1, 3):
+            if k != 2:
 
                 @pl.when(jnp.logical_not(sends[side]))
                 def _():
-                    for piece in ((0, 1), (2,))[k // 2]:
-                        for copy in edge_copies(side, piece):
-                            copy.start()
+                    for copy in edge_copies(side, ((0, 1, 2), (1, 0, 2))[side][k - k // 2]):
+                        copy.start()
 
     gather_near((0, 1, 2), False)
 

time: 81.6 us -> 80.7 us (0.989)
  Pallas kernels: 77.3 us -> 76.4 us
    pallas_call x1, Pallas kernels: 77.3 us -> 76.4 us  [body(): pl.pallas_call(kernel, out_shape=(jax.ShapeDtypeStruct((1, 1024, 512), bf...]
where the time goes in v6:
time: 80.7 us; the launch traced here: 80.6 us
  Pallas kernels  76.4 us (95%)
  between operations  2.58 us (3%)
  local copies, waits for them, and re-layouts  1.56 us (2%)
    pallas_call x1, Pallas kernels, body(): pl.pallas_call(kernel, out_shape=(jax.ShapeDtypeStruct((1, 1024, 512), bf...  76.4 us

profile of v6, /device:TPU:1, one launch (start us, length us, event | category | flops | bytes accessed | tf_op | source)
XLA Modules:
  0.0 80.6 jit_solution(13822149772223829578)
XLA Ops:
  2.6 76.4 %langevin_step.1 = (bf16[1,1024,512]{2,1,0:T(8,128)(2,1)S(1)}, f32[1,2,512]{2,1,0:T(2,128)S(1)}) custom-call(bf16[384,1024]{1,0:T(8,128)(2,1)} %res_hbm.1, bf16[1,1024,512]{2,1,0:T(8,128)(2,1)} %par_hbm.1, bf16[1,1024,512]{2,1,0:T(8,128)(2,1)} %noise_hbm.1, bf16[512,1024]{1,0:T(8,128)(2,1)} %down_hbm.1, f32[1]{0:T(128)S(6)} %copy.11.heat, s32[1]{0:T(128)S(6)} %copy.12.mate, ...), custom_call_target="tpu_custom_call" | custom-call | tf_op jit(solution)/shard_map/langevin_step/pallas_call | solution.py:524
  79.0 1.0 %copy.14 = bf16[1,1024,512]{2,1,0:T(8,128)(2,1)} copy(bf16[1,1024,512]{2,1,0:T(8,128)(2,1)S(1)} %get-tuple-element.4) | data formatting | bytes 2097152
  80.0 0.6 copy.15
